TPU v7x, 32 devices: a whole 2x2x4 slice. The times are simulated.
32 devices in a mesh: seq: 4 (over z), shard: 8 (over y, x, core).
Axes of the slice: x: 2, y: 2, z: 4, core: 2. Of those that a mesh axis runs over, the one named last changes fastest.
Arguments:
- frames: bfloat16 [8, 1024, 1536], P('shard', 'seq'), may hold values from -6 to 6
- text_states: bfloat16 [8, 64, 1536], P('shard'), may hold values from -6 to 6
- norm_gain: bfloat16 [3, 1536], P(None, 'shard'), may hold values from 0.5 to 1.5
- norm_bias: bfloat16 [3, 1536], P(None, 'shard'), may hold values from -3 to 3
- self_project: bfloat16 [3, 1536, 1536], P(None, 'shard'), may hold values from -0.15625 to 0.15625
- self_output: bfloat16 [1536, 1536], P('shard'), may hold values from -1.75 to 1.75
- cross_project: bfloat16 [3, 1536, 1536], P(None, 'shard'), may hold values from -0.15625 to 0.15625
- cross_output: bfloat16 [1536, 1536], P('shard'), may hold values from -0.625 to 0.625
- up_weight: bfloat16 [1536, 6144], P('shard'), may hold values from -0.15625 to 0.15625
- down_weight: bfloat16 [6144, 1536], P('shard'), may hold values from -0.078125 to 0.078125
- cotangent: bfloat16 [8, 1024, 1536], P('shard', 'seq'), may hold values from -6 to 6
Outputs:
- output: bfloat16 [8, 1024, 1536], P('shard', 'seq')
- frames_grad: float32 [8, 1024, 1536], P('shard', 'seq')
- text_grad: float32 [8, 64, 1536], P('shard')
- gain_grad: float32 [3, 1536], P(None, 'shard')
- bias_grad: float32 [3, 1536], P(None, 'shard')
- self_project_grad: float32 [3, 1536, 1536], P(None, 'shard')
- self_output_grad: float32 [1536, 1536], P('shard')
- cross_project_grad: float32 [3, 1536, 1536], P(None, 'shard')
- cross_output_grad: float32 [1536, 1536], P('shard')
- up_grad: float32 [1536, 6144], P('shard')
- down_grad: float32 [6144, 1536], P('shard')
All inputs are finite; a program needn't handle non-finite values.
Results may differ from a plain program's by a relative error of at most 0.022.
Values may be sent and summed in bfloat16 or wider, within the bound.
No kernel may reach another device: no remote copies, remote signals or barrier semaphores. Data moves between devices by JAX's collectives and lax.ppermute only.
A program may use at most 384 MiB of HBM per device.

v0:
```python
import jax
import jax.numpy as jnp
from jax import lax
from jax.sharding import PartitionSpec as P

HEAD_DIM = 64
QBLOCK = 512
EPSILON = 1e-05
MASKED_SCORE = -1e30


def layer_norm(hidden, gain, shift):
    center = hidden - jnp.mean(hidden, axis=-1, keepdims=True)
    spread = lax.rsqrt(jnp.mean(center * center, axis=-1, keepdims=True) + EPSILON)
    return center * spread * gain + shift


def exact_gelu(values):
    return jax.nn.gelu(values, approximate=False)


def contract(form, left, right):
    return jnp.einsum(form, left, right, preferred_element_type=jnp.float32)


def split_heads(values):
    return values.reshape(values.shape[:-1] + (values.shape[-1] // HEAD_DIM, HEAD_DIM))


def join_heads(values):
    return values.reshape(values.shape[:-2] + (values.shape[-2] * values.shape[-1],))


def causal_visible(start_row, row_count, stop_row):
    row_place = start_row + lax.broadcasted_iota(jnp.int32, (row_count, stop_row), 0)
    column_place = lax.broadcasted_iota(jnp.int32, (row_count, stop_row), 1)
    return column_place <= row_place


def block_scores(queries, key_rows, start_row, stop_row, scaling):
    scores = (
        contract("cqhe,ckhe->chqk", queries[:, start_row:stop_row], key_rows[:, :stop_row])
        * scaling
    )
    return jnp.where(
        causal_visible(start_row, stop_row - start_row, stop_row), scores, MASKED_SCORE
    )


def self_forward(queries, key_rows, value_rows, scaling):
    length = queries.shape[1]
    outputs = []
    totals = []
    for start_row in range(0, length, QBLOCK):
        stop_row = start_row + QBLOCK
        scores = block_scores(queries, key_rows, start_row, stop_row, scaling)
        largest = jnp.max(scores, axis=-1, keepdims=True)
        weights = jnp.exp(scores - largest)
        summed = jnp.sum(weights, axis=-1, keepdims=True)
        shares = (weights / summed).astype(jnp.bfloat16)
        outputs.append(contract("chqk,ckhe->cqhe", shares, value_rows[:, :stop_row]))
        totals.append(largest + jnp.log(summed))
    return (jnp.concatenate(outputs, axis=1), totals)


def self_backward(queries, key_rows, value_rows, totals, grad_out, scaling):
    length = queries.shape[1]
    grad_queries = []
    grad_keys = jnp.zeros(key_rows.shape, jnp.float32)
    grad_values = jnp.zeros(value_rows.shape, jnp.float32)
    for number, start_row in enumerate(range(0, length, QBLOCK)):
        stop_row = start_row + QBLOCK
        query_block = queries[:, start_row:stop_row]
        grad_block = grad_out[:, start_row:stop_row]
        scores = block_scores(queries, key_rows, start_row, stop_row, scaling)
        shares = jnp.exp(scores - totals[number])
        grad_shares = contract("cqhe,ckhe->chqk", grad_block, value_rows[:, :stop_row])
        centred = jnp.sum(shares * grad_shares, axis=-1, keepdims=True)
        grad_scores = (shares * (grad_shares - centred)).astype(jnp.bfloat16)
        grad_queries.append(
            contract("chqk,ckhe->cqhe", grad_scores, key_rows[:, :stop_row]) * scaling
        )
        grad_keys = grad_keys.at[:, :stop_row].add(
            contract("chqk,cqhe->ckhe", grad_scores, query_block) * scaling
        )
        grad_values = grad_values.at[:, :stop_row].add(
            contract("chqk,cqhe->ckhe", shares.astype(jnp.bfloat16), grad_block)
        )
    return (jnp.concatenate(grad_queries, axis=1), grad_keys, grad_values)


def cross_softmax(queries, key_rows, scaling):
    scores = contract("cfhe,cxhe->chxf", queries, key_rows) * scaling
    largest = jnp.max(scores, axis=2, keepdims=True)
    weights = jnp.exp(scores - largest)
    return weights / jnp.sum(weights, axis=2, keepdims=True)


def fetch_self(self_project, self_output, norm_gain, norm_bias):
    return (
        lax.all_gather(self_project, "shard", axis=1, tiled=True),
        lax.all_gather(self_output, "shard", axis=0, tiled=True),
        lax.all_gather(norm_gain, "shard", axis=1, tiled=True),
        lax.all_gather(norm_bias, "shard", axis=1, tiled=True),
    )


def fetch_cross(cross_project, cross_output):
    return (
        lax.all_gather(cross_project, "shard", axis=1, tiled=True),
        lax.all_gather(cross_output, "shard", axis=0, tiled=True),
    )


def fetch_mlp(up_weight, down_weight):
    return (
        lax.all_gather(up_weight, "shard", axis=0, tiled=True),
        lax.all_gather(down_weight, "shard", axis=0, tiled=True),
    )


def body(
    frames,
    text_states,
    norm_gain,
    norm_bias,
    self_project,
    self_output,
    cross_project,
    cross_output,
    up_weight,
    down_weight,
    cotangent,
):
    scaling = HEAD_DIM ** (-0.5)
    project_all, output_all, gain_all, bias_all = fetch_self(
        self_project, self_output, norm_gain, norm_bias
    )
    gains = gain_all.astype(jnp.float32)
    biases = bias_all.astype(jnp.float32)
    hidden = frames.astype(jnp.float32)
    normed_one, norm_pull_one = jax.vjp(layer_norm, hidden, gains[0], biases[0])
    inputs_one = normed_one.astype(jnp.bfloat16)
    projected = contract("cfd,jde->jcfe", inputs_one, project_all).astype(jnp.bfloat16)
    by_heads = lax.all_to_all(projected, "seq", split_axis=3, concat_axis=2, tiled=True)
    queries = split_heads(by_heads[0])
    key_rows = split_heads(by_heads[1])
    value_rows = split_heads(by_heads[2])
    attended_heads, totals = self_forward(queries, key_rows, value_rows, scaling)
    attended = lax.all_to_all(
        join_heads(attended_heads).astype(jnp.bfloat16),
        "seq",
        split_axis=1,
        concat_axis=2,
        tiled=True,
    )
    hidden_one = hidden + contract("cfd,de->cfe", attended, output_all)
    cross_all, cross_out_all = fetch_cross(cross_project, cross_output)
    normed_two, norm_pull_two = jax.vjp(layer_norm, hidden_one, gains[1], biases[1])
    inputs_two = normed_two.astype(jnp.bfloat16)
    cross_queries = contract("cfd,de->cfe", inputs_two, cross_all[0]).astype(jnp.bfloat16)
    cross_pairs = contract("cxd,jde->jcxe", text_states, cross_all[1:]).astype(jnp.bfloat16)
    text_keys = split_heads(cross_pairs[0])
    text_values = split_heads(cross_pairs[1])
    cross_shares = cross_softmax(split_heads(cross_queries), text_keys, scaling)
    cross_low = cross_shares.astype(jnp.bfloat16)
    mixed_text = join_heads(contract("chxf,cxhe->cfhe", cross_low, text_values)).astype(
        jnp.bfloat16
    )
    hidden_two = hidden_one + contract("cfd,de->cfe", mixed_text, cross_out_all)
    up_all, down_all = fetch_mlp(up_weight, down_weight)
    normed_three, norm_pull_three = jax.vjp(layer_norm, hidden_two, gains[2], biases[2])
    inputs_three = normed_three.astype(jnp.bfloat16)
    before_act = contract("cfd,dk->cfk", inputs_three, up_all)
    activated, gelu_pull = jax.vjp(exact_gelu, before_act)
    activated_low = activated.astype(jnp.bfloat16)
    result = hidden_two + contract("cfk,kd->cfd", activated_low, down_all)
    output = result.astype(jnp.bfloat16)
    up_all, down_all = fetch_mlp(up_weight, down_weight)
    grad_result = cotangent.astype(jnp.float32)
    grad_down = contract("cfk,cfd->kd", activated_low, cotangent)
    grad_act = contract("cfd,kd->cfk", cotangent, down_all)
    grad_before = gelu_pull(grad_act)[0].astype(jnp.bfloat16)
    grad_up = contract("cfd,cfk->dk", inputs_three, grad_before)
    grad_inputs_three = contract("cfk,dk->cfd", grad_before, up_all)
    grad_two_part, gain_three, bias_three = norm_pull_three(grad_inputs_three)
    grad_hidden_two = grad_result + grad_two_part
    up_share, down_share = (
        lax.psum_scatter(
            grad_up.astype(jnp.bfloat16), "shard", scatter_dimension=0, tiled=True
        ).astype(jnp.float32),
        lax.psum_scatter(
            grad_down.astype(jnp.bfloat16), "shard", scatter_dimension=0, tiled=True
        ).astype(jnp.float32),
    )
    cross_all, cross_out_all = fetch_cross(cross_project, cross_output)
    grad_low_two = grad_hidden_two.astype(jnp.bfloat16)
    grad_cross_out = contract("cfd,cfe->de", mixed_text, grad_low_two)
    grad_mixed = split_heads(
        contract("cfe,de->cfd", grad_low_two, cross_out_all).astype(jnp.bfloat16)
    )
    grad_shares = contract("cfhe,cxhe->chxf", grad_mixed, text_values)
    centred = jnp.sum(cross_shares * grad_shares, axis=2, keepdims=True)
    grad_scores = (cross_shares * (grad_shares - centred)).astype(jnp.bfloat16)
    grad_cross_query = join_heads(
        contract("chxf,cxhe->cfhe", grad_scores, text_keys) * scaling
    ).astype(jnp.bfloat16)
    grad_text_keys = join_heads(
        contract("chxf,cfhe->cxhe", grad_scores, split_heads(cross_queries)) * scaling
    )
    grad_text_values = join_heads(contract("chxf,cfhe->cxhe", cross_low, grad_mixed))
    grad_pairs = lax.psum(jnp.stack([grad_text_keys, grad_text_values]).astype(jnp.bfloat16), "seq")
    grad_text = contract("jcxe,jde->cxd", grad_pairs, cross_all[1:])
    grad_cross_pairs = contract("cxd,jcxe->jde", text_states, grad_pairs)
    grad_cross_first = contract("cfd,cfe->de", inputs_two, grad_cross_query)
    grad_inputs_two = contract("cfe,de->cfd", grad_cross_query, cross_all[0])
    grad_one_part, gain_two, bias_two = norm_pull_two(grad_inputs_two)
    grad_hidden_one = grad_hidden_two + grad_one_part
    cross_stack = jnp.concatenate([grad_cross_first[None], grad_cross_pairs], axis=0)
    cross_share, cross_out_share = (
        lax.psum_scatter(
            cross_stack.astype(jnp.bfloat16), "shard", scatter_dimension=1, tiled=True
        ).astype(jnp.float32),
        lax.psum_scatter(
            grad_cross_out.astype(jnp.bfloat16), "shard", scatter_dimension=0, tiled=True
        ).astype(jnp.float32),
    )
    project_all, output_all, gain_all, bias_all = fetch_self(
        self_project, self_output, norm_gain, norm_bias
    )
    grad_low_one = grad_hidden_one.astype(jnp.bfloat16)
    grad_self_out = contract("cfd,cfe->de", attended, grad_low_one)
    grad_attended = contract("cfe,de->cfd", grad_low_one, output_all).astype(jnp.bfloat16)
    grad_heads = lax.all_to_all(grad_attended, "seq", split_axis=2, concat_axis=1, tiled=True)
    grad_queries, grad_keys, grad_values = self_backward(
        queries, key_rows, value_rows, totals, split_heads(grad_heads), scaling
    )
    grad_stacked = jnp.stack(
        [join_heads(grad_queries), join_heads(grad_keys), join_heads(grad_values)]
    ).astype(jnp.bfloat16)
    grad_projected = lax.all_to_all(grad_stacked, "seq", split_axis=2, concat_axis=3, tiled=True)
    grad_self_project = contract("cfd,jcfe->jde", inputs_one, grad_projected)
    grad_inputs_one = contract("jcfe,jde->cfd", grad_projected, project_all)
    grad_zero_part, gain_one, bias_one = norm_pull_one(grad_inputs_one)
    grad_frames = grad_hidden_one + grad_zero_part
    gain_stack = jnp.stack([gain_one, gain_two, gain_three])
    bias_stack = jnp.stack([bias_one, bias_two, bias_three])
    project_share, output_share, gain_share, bias_share = (
        lax.psum_scatter(
            grad_self_project.astype(jnp.bfloat16), "shard", scatter_dimension=1, tiled=True
        ).astype(jnp.float32),
        lax.psum_scatter(
            grad_self_out.astype(jnp.bfloat16), "shard", scatter_dimension=0, tiled=True
        ).astype(jnp.float32),
        lax.psum_scatter(
            gain_stack.astype(jnp.bfloat16), "shard", scatter_dimension=1, tiled=True
        ).astype(jnp.float32),
        lax.psum_scatter(
            bias_stack.astype(jnp.bfloat16), "shard", scatter_dimension=1, tiled=True
        ).astype(jnp.float32),
    )
    summed_parts = (
        lax.psum(project_share.astype(jnp.bfloat16), "seq").astype(jnp.float32),
        lax.psum(output_share.astype(jnp.bfloat16), "seq").astype(jnp.float32),
        lax.psum(cross_share[:1].astype(jnp.bfloat16), "seq").astype(jnp.float32),
        lax.psum(cross_out_share.astype(jnp.bfloat16), "seq").astype(jnp.float32),
        lax.psum(up_share.astype(jnp.bfloat16), "seq").astype(jnp.float32),
        lax.psum(down_share.astype(jnp.bfloat16), "seq").astype(jnp.float32),
        lax.psum(gain_share.astype(jnp.bfloat16), "seq").astype(jnp.float32),
        lax.psum(bias_share.astype(jnp.bfloat16), "seq").astype(jnp.float32),
    )
    cross_final = jnp.concatenate([summed_parts[2], cross_share[1:]], axis=0)
    return (
        output,
        grad_frames,
        grad_text,
        summed_parts[6],
        summed_parts[7],
        summed_parts[0],
        summed_parts[1],
        cross_final,
        summed_parts[3],
        summed_parts[4],
        summed_parts[5],
    )


def solution(mesh):
    return jax.shard_map(
        body,
        mesh=mesh,
        in_specs=(
            P("shard", "seq", None),
            P("shard", None, None),
            P(None, "shard"),
            P(None, "shard"),
            P(None, "shard", None),
            P("shard", None),
            P(None, "shard", None),
            P("shard", None),
            P("shard", None),
            P("shard", None),
            P("shard", "seq", None),
        ),
        out_specs=(
            P("shard", "seq", None),
            P("shard", "seq", None),
            P("shard", None, None),
            P(None, "shard"),
            P(None, "shard"),
            P(None, "shard", None),
            P("shard", None),
            P(None, "shard", None),
            P("shard", None),
            P("shard", None),
            P("shard", None),
        ),
        check_vma=False,
    )
```

profile of v0, /device:TPU:0, one launch (start us, length us, event | category | flops | bytes accessed | tf_op | source)
XLA Modules:
  0.0 1739.3 jit_solution(10451731953631284153)
XLA Ops:
  11.2 10.4 all-gather
  21.7 9.2 all-gather.1
  31.7 59.6 %all-gather.9.cloned.1.call-done = bf16[3,1536,1536]{2,1,0:T(8,128)(2,1)} async-done(((bf16[3,192,1536]{2,1,0:T(8,128)(2,1)}), bf16[3,1536,1536]{2,1,0:T(8,128)(2,1)}) %all-gather.9.cloned.1.call-update) | async-done | bytes 14155792 | tf_op jit(solution)/shard_map/all_gather | solution.py:101
  91.4 9.3 fusion.27
  111.2 69.5 %all-to-all-done = bf16[3,1,256,1536]{2,0,1,3:T(4,128)(2,1)} async-done(((bf16[3,1,256,1536]{2,0,1,3:T(4,128)(2,1)}), bf16[3,1,256,1536]{2,0,1,3:T(4,128)(2,1)}, u32[]{:S(2)}, u32[]{:S(2)}) %all-to-all-start) | async-done | bytes 2359328 | tf_op jit(solution)/shard_map/all_to_all | solution.py:145
  228.0 11.9 all-to-all-done.1
  261.1 92.5 %all-gather.17.cloned.1.call-done = bf16[1536,6144]{1,0:T(8,128)(2,1)} async-done(((bf16[192,6144]{1,0:T(8,128)(2,1)}), bf16[1536,6144]{1,0:T(8,128)(2,1)}) %all-gather.17.cloned.1.call-update) | async-done | bytes 18874384 | tf_op jit(solution)/shard_map/all_gather | solution.py:117
  353.6 23.7 %multiply_convert_fusion.2 = (bf16[256,6144]{1,0:T(8,128)(2,1)}, f32[256,6144]{1,0:T(8,128)}, f32[256,6144]{1,0:T(8,128)}) fusion(bf16[1536,6144]{1,0:T(8,128)(2,1)} %all-gather.17.cloned.1.call-done, f32[1,256,1536]{2,1,0:T(8,128)S(1)} %get-tuple-element.192, f32[1536]{0:T(1024)S(1)} %get-tuple-element.161, f32[1536]{0:T(1024)S(1)} %get-tuple-element.206, ...), kind=kOutput, calls=%fused_computation.31 | convolution fusion | flops 4936040448 | bytes 36190208 | tf_op jit(solution)/shard_map/cfd,dk->cfk/dot_general | solution.py:23
  377.3 76.7 %all-gather.19.cloned.1.call-done = bf16[6144,1536]{1,0:T(8,128)(2,1)} async-done(((bf16[768,1536]{1,0:T(8,128)(2,1)}), bf16[6144,1536]{1,0:T(8,128)(2,1)}) %all-gather.19.cloned.1.call-update) | async-done | bytes 18874384 | tf_op jit(solution)/shard_map/all_gather | solution.py:118
  453.9 14.8 add_convert_fusion
  468.7 10.7 fusion.57
  513.5 24.0 %all-reduce.7.cloned.1.call-done = bf16[2,64,1536]{2,1,0:T(8,128)(2,1)} async-done(((bf16[2,64,1536]{2,1,0:T(8,128)(2,1)}), bf16[2,64,1536]{2,1,0:T(8,128)(2,1)}) %all-reduce.7.cloned.1.call-update) | async-done | bytes 393232 | tf_op jit(solution)/shard_map/psum | solution.py:212
  547.7 30.8 %copy.225 = bf16[3,1536,1536]{2,0,1:T(4,128)(2,1)} copy(bf16[3,1536,1536]{1,2,0:T(8,128)(2,1)} %pad_maximum_fusion) | data formatting | bytes 28311552
  578.5 17.0 copy.233
  607.5 8.2 reduce.60
  620.5 18.2 %all-to-all-done.2 = bf16[4,2,49152]{2,1,0:T(2,128)(2,1)S(1)} async-done(((bf16[4,2,49152]{2,1,0:T(2,128)(2,1)}), bf16[4,2,49152]{2,1,0:T(2,128)(2,1)S(1)}, u32[]{:S(2)}, u32[]{:S(2)}) %all-to-all-start.2) | async-done | bytes 786464 | tf_op jit(solution)/shard_map/all_to_all | solution.py:234
  709.7 72.8 %all_to_all.60 = bf16[3,1,1024,384]{3,0,1,2:T(4,128)(2,1)S(1)} all-to-all(bf16[3,1,1024,384]{3,0,1,2:T(4,128)(2,1)S(1)} %pad_maximum_fusion.1), channel_id=1, replica_groups=mesh['seq'=4,'shard'=8] {'seq'}, dimensions={2} | all-to-all | bytes 4718592 | tf_op jit(solution)/shard_map/all_to_all | solution.py:241
  797.7 30.8 %copy.223 = bf16[3,1536,1536]{2,0,1:T(4,128)(2,1)} copy(bf16[3,1536,1536]{1,2,0:T(8,128)(2,1)} %convert_bitcast_fusion) | data formatting | bytes 28311552
  828.6 17.0 copy.232
  858.2 12.6 convolution_convert_fusion.1
  870.9 11.4 convolution_convert_fusion
  906.5 40.3 %reduce-scatter.29.cloned.1.call-done = bf16[192,4608]{1,0:T(8,128)(2,1)} async-done(((bf16[1536,4608]{1,0:T(8,128)(2,1)}), bf16[192,4608]{1,0:T(8,128)(2,1)}) %reduce-scatter.29.cloned.1.call-update) | async-done | bytes 1769488
  957.5 46.9 %reduce-scatter.19.cloned.1.call-done = bf16[192,1536]{1,0:T(8,128)(2,1)} async-done(((bf16[1536,1536]{1,0:T(8,128)(2,1)}), bf16[192,1536]{1,0:T(8,128)(2,1)}) %reduce-scatter.19.cloned.1.call-update) | async-done | bytes 589840 | tf_op jit(solution)/shard_map/reduce_scatter | solution.py:224
  1004.5 57.8 %reduce-scatter.17.cloned.1.call-done = bf16[192,1536]{1,0:T(8,128)(2,1)} async-done(((bf16[1536,1536]{1,0:T(8,128)(2,1)}), bf16[192,1536]{1,0:T(8,128)(2,1)}) %reduce-scatter.17.cloned.1.call-update) | async-done | bytes 589840 | tf_op jit(solution)/shard_map/reduce_scatter | solution.py:252
  1062.3 129.9 %reduce-scatter.21.cloned.1.call-done = bf16[192,6144]{1,0:T(8,128)(2,1)} async-done(((bf16[1536,6144]{1,0:T(8,128)(2,1)}), bf16[192,6144]{1,0:T(8,128)(2,1)}) %reduce-scatter.21.cloned.1.call-update) | async-done | bytes 2359312 | tf_op jit(solution)/shard_map/reduce_scatter | solution.py:189
  1192.2 130.1 %reduce-scatter.23.cloned.1.call-done = bf16[768,1536]{1,0:T(8,128)(2,1)} async-done(((bf16[6144,1536]{1,0:T(8,128)(2,1)}), bf16[768,1536]{1,0:T(8,128)(2,1)}) %reduce-scatter.23.cloned.1.call-update) | async-done | bytes 2359312 | tf_op jit(solution)/shard_map/reduce_scatter | solution.py:192
  1323.7 10.7 fusion.31
  1334.4 7.6 fusion.44
  1343.7 15.4 reduce-scatter.25.cloned.1.call-done
  1360.0 35.9 %reduce-scatter.27.cloned.1.call-done = bf16[192,3]{1,0:T(8,128)(2,1)} async-done(((bf16[1536,3]{1,0:T(8,128)(2,1)}), bf16[192,3]{1,0:T(8,128)(2,1)}) %reduce-scatter.27.cloned.1.call-update) | async-done | bytes 1168
  1396.8 11.9 all-reduce.2
  1414.7 297.1 %all-reduce.9.cloned.1.call-done = (bf16[3,192,1536]{1,2,0:T(8,128)(2,1)}, bf16[192,1536]{1,0:T(8,128)(2,1)}, bf16[1,192,1536]{1,2,0:T(8,128)(2,1)}, bf16[192,15...) async-done(((bf16[3,192,1536]{1,2,0:T(8,128)(2,1)}, bf16[192,1536]{1,0:T(8,128)(2,1)}, bf16[1,192,1536]{1,2,0:T(8,128)(2,1)}, ...) | async-done | bytes 8257552 | tf_op jit(solution)/shard_map/psum | solution.py:263
  (372 shorter events, 308.8 us)
Async XLA Ops:
  7.2 212.9 %copy-start = (bf16[1,64,1536]{2,1,0:T(8,128)(2,1)S(1)}, bf16[1,64,1536]{2,1,0:T(8,128)(2,1)}, u32[]{:S(2)}) copy-start(bf16[1,64,1536]{2,1,0:T(8,128)(2,1)} %param.24) | copy-start | bytes 589828
  7.2 84.2 %all-gather.9.cloned.1.call-start = ((), (), s32[]{:S(2)}) async-start(), calls=%async_computation.12 | async-start | bytes 15925248 | tf_op jit(solution)/shard_map/all_gather | solution.py:101
  7.9 212.1 %all-gather.13.cloned.1.call-start = ((), (), s32[]{:S(2)}) async-start(), calls=%async_computation.14 | async-start | bytes 15925248 | tf_op jit(solution)/shard_map/all_gather | solution.py:110
  8.7 232.6 %all-gather.11.cloned.1.call-start = ((), (), s32[]{:S(2)}) async-start(), calls=%async_computation.13 | async-start | bytes 5308416 | tf_op jit(solution)/shard_map/all_gather | solution.py:102
  9.4 247.2 %all-gather.15.cloned.1.call-start = ((), (), s32[]{:S(2)}) async-start(), calls=%async_computation.15 | async-start | bytes 5308416 | tf_op jit(solution)/shard_map/all_gather | solution.py:111
  10.0 343.6 %all-gather.17.cloned.1.call-start = ((), (), s32[]{:S(2)}) async-start(), calls=%async_computation.16 | async-start | bytes 21233664 | tf_op jit(solution)/shard_map/all_gather | solution.py:117
  10.6 443.3 %all-gather.19.cloned.1.call-start = ((), (), s32[]{:S(2)}) async-start(), calls=%async_computation.17 | async-start | bytes 21233664 | tf_op jit(solution)/shard_map/all_gather | solution.py:118
  31.1 69.6 %copy-start.54 = (f32[1536]{0:T(1024)}, f32[1536]{0:T(1024)S(1)}, u32[]{:S(2)}) copy-start(f32[1536]{0:T(1024)S(1)} %get-tuple-element.204) | copy-start | bytes 18436
  31.1 69.6 %copy-start.65 = (f32[1536]{0:T(1024)}, f32[1536]{0:T(1024)S(1)}, u32[]{:S(2)}) copy-start(f32[1536]{0:T(1024)S(1)} %get-tuple-element.163) | copy-start | bytes 18436
  31.1 214.7 %copy-start.67 = (f32[1536]{0:T(1024)}, f32[1536]{0:T(1024)S(1)}, u32[]{:S(2)}) copy-start(f32[1536]{0:T(1024)S(1)} %get-tuple-element.205) | copy-start | bytes 18436
  31.1 214.7 %copy-start.83 = (f32[1536]{0:T(1024)}, f32[1536]{0:T(1024)S(1)}, u32[]{:S(2)}) copy-start(f32[1536]{0:T(1024)S(1)} %get-tuple-element.162) | copy-start | bytes 18436
  31.1 322.4 %copy-start.56 = (f32[1536]{0:T(1024)}, f32[1536]{0:T(1024)S(1)}, u32[]{:S(2)}) copy-start(f32[1536]{0:T(1024)S(1)} %get-tuple-element.161) | copy-start | bytes 18436
  31.4 69.4 %copy-start.70 = (f32[256]{0:T(256)}, f32[256]{0:T(256)S(1)}, u32[]{:S(2)}) copy-start(f32[256]{0:T(256)S(1)} %broadcast_multiply_fusion.2) | copy-start | bytes 3076
  31.7 69.0 %copy-start.76 = (f32[256]{0:T(256)}, f32[256]{0:T(256)S(1)}, u32[]{:S(2)}) copy-start(f32[256]{0:T(256)S(1)} %fusion.53) | copy-start | bytes 3076
  31.7 69.0 %copy-start.72 = (f32[256]{0:T(256)}, f32[256]{0:T(256)S(1)}, u32[]{:S(2)}) copy-start(f32[256]{0:T(256)S(1)} %fusion.100) | copy-start | bytes 3076
  104.3 76.4 %all-to-all-start = ((bf16[3,1,256,1536]{2,0,1,3:T(4,128)(2,1)}), bf16[3,1,256,1536]{2,0,1,3:T(4,128)(2,1)}, u32[]{:S(2)}, u32[]{:S(2)}) async-start(bf16[3,1,256,1536]{2,0,1,3:T(4,128)(2,1)} %copy.187), calls=%async_computation | async-start | bytes 6291456 | tf_op jit(solution)/shard_map/all_to_all | solution.py:145
  216.4 23.5 %all-to-all-start.1 = ((bf16[4,2,49152]{2,1,0:T(2,128)(2,1)}), bf16[4,2,49152]{2,1,0:T(2,128)(2,1)S(1)}, u32[]{:S(2)}, u32[]{:S(2)}) async-start(bf16[4,2,49152]{2,1,0:T(2,128)(2,1)} %reshape.954), calls=%async_computation.1 | async-start | bytes 1572864 | tf_op jit(solution)/shard_map/all_to_all | solution.py:150
  220.0 317.6 %all-reduce.7.cloned.1.call-start = ((), (), s32[]{:S(2)}) async-start(), calls=%async_computation.18 | async-start | bytes 786432 | tf_op jit(solution)/shard_map/psum | solution.py:212
  254.0 237.8 %copy-start.58 = (f32[24,256]{1,0:T(8,128)}, f32[24,256]{1,0:T(8,128)S(1)}, u32[]{:S(2)}) copy-start(f32[24,256]{1,0:T(8,128)S(1)} %get-tuple-element.189) | copy-start | bytes 73732
  260.8 218.7 %copy-start.9 = (f32[1,256,1536]{2,1,0:T(8,128)}, f32[1,256,1536]{2,1,0:T(8,128)S(1)}, u32[]{:S(2)}) copy-start(f32[1,256,1536]{2,1,0:T(8,128)S(1)} %get-tuple-element.192) | copy-start | bytes 4718596
  500.4 396.8 %reduce-scatter.31.cloned.1.call-start = ((), (), s32[]{:S(2)}) async-start(), calls=%async_computation.26 | async-start | bytes 15925248
  616.7 22.0 %all-to-all-start.2 = ((bf16[4,2,49152]{2,1,0:T(2,128)(2,1)}), bf16[4,2,49152]{2,1,0:T(2,128)(2,1)S(1)}, u32[]{:S(2)}, u32[]{:S(2)}) async-start(bf16[4,2,49152]{2,1,0:T(2,128)(2,1)} %reshape.956), calls=%async_computation.2 | async-start | bytes 1572864 | tf_op jit(solution)/shard_map/all_to_all | solution.py:234
  620.5 326.3 %reduce-scatter.29.cloned.1.call-start = ((), (), s32[]{:S(2)}) async-start(), calls=%async_computation.25 | async-start | bytes 15925248
  845.6 158.8 %reduce-scatter.19.cloned.1.call-start = ((), (), s32[]{:S(2)}) async-start(), calls=%async_computation.20 | async-start | bytes 5308416 | tf_op jit(solution)/shard_map/reduce_scatter | solution.py:224
  851.5 210.8 %reduce-scatter.17.cloned.1.call-start = ((), (), s32[]{:S(2)}) async-start(), calls=%async_computation.19 | async-start | bytes 5308416 | tf_op jit(solution)/shard_map/reduce_scatter | solution.py:252
  857.6 334.7 %reduce-scatter.21.cloned.1.call-start = ((), (), s32[]{:S(2)}) async-start(), calls=%async_computation.21 | async-start | bytes 21233664 | tf_op jit(solution)/shard_map/reduce_scatter | solution.py:189
  870.8 451.5 %reduce-scatter.23.cloned.1.call-start = ((), (), s32[]{:S(2)}) async-start(), calls=%async_computation.22 | async-start | bytes 21233664 | tf_op jit(solution)/shard_map/reduce_scatter | solution.py:192
  882.3 476.8 %reduce-scatter.25.cloned.1.call-start = ((), (), s32[]{:S(2)}) async-start(), calls=%async_computation.23 | async-start | bytes 442368
  895.9 500.1 %reduce-scatter.27.cloned.1.call-start = ((), (), s32[]{:S(2)}) async-start(), calls=%async_computation.24 | async-start | bytes 442368
  897.0 814.8 %all-reduce.9.cloned.1.call-start = ((), (), s32[]{:S(2)}) async-start(), calls=%async_computation.27 | async-start | bytes 18087936 | tf_op jit(solution)/shard_map/psum | solution.py:263
  901.0 50.9 %copy-start.17 = (bf16[192,3,1536]{2,1,0:T(4,128)(2,1)}, bf16[192,3,1536]{2,1,0:T(4,128)(2,1)S(1)}, u32[]{:S(2)}) copy-start(bf16[192,3,1536]{2,1,0:T(4,128)(2,1)S(1)} %reshape.947) | copy-start | bytes 5308420
  1342.0 67.9 %copy-start.18 = (bf16[192,3,1536]{2,1,0:T(4,128)(2,1)S(1)}, bf16[192,3,1536]{2,1,0:T(4,128)(2,1)}, u32[]{:S(2)}) copy-start(bf16[192,3,1536]{2,1,0:T(4,128)(2,1)} %copy-done.17) | copy-start | bytes 5308420
  (83 other events, 440.9 us)
Sparse Core Ops, SparseCore 0:
  9.9 81.4 all-gather.8
  93.3 78.6 all-gather.12
  173.8 38.7 all-gather.10
  214.4 38.7 all-gather.14
  255.0 98.5 all-gather.16
  355.3 98.5 all-gather.18
  500.6 36.9 all-reduce.6
  595.7 101.5 reduce-scatter.30
  845.8 100.9 reduce-scatter.28
  950.6 53.7 reduce-scatter.18
  1008.5 53.7 reduce-scatter.16
  1065.8 126.4 reduce-scatter.20
  1195.8 126.4 reduce-scatter.22
  1325.2 33.8 reduce-scatter.24
  1362.0 33.8 reduce-scatter.26
  1399.6 312.1 all-reduce.8
where the time goes:
time: 1750 us; the launch traced here: 1740 us
  waiting for transfers between devices  1110 us (63%)
  matrix products  220 us (13%)
  local copies, waits for them, and re-layouts  207 us (12%)
  blocking collectives  104 us (6%)
  other arithmetic  70.1 us (4%)
    psum x1, waiting for transfers between devices, body(): lax.psum(project_share.astype(jnp.bfloat16), 'seq').astype(jnp.float32)  297 us
    dot_general x38, matrix products, contract(): return jnp.einsum(form, left, right, preferred_element_type=jnp.float32)  218 us
    unnamed x214, local copies, waits for them, and re-layouts  146 us
    reduce_scatter x1, waiting for transfers between devices, body(): lax.psum_scatter(grad_down.astype(jnp.bfloat16), 'shard', scatter_dimensi...  130 us
    reduce_scatter x1, waiting for transfers between devices, body(): lax.psum_scatter(grad_up.astype(jnp.bfloat16), 'shard', scatter_dimension...  130 us
    unnamed x20, waiting for transfers between devices  95.5 us
    all_gather x1, waiting for transfers between devices, fetch_mlp(): lax.all_gather(up_weight, 'shard', axis=0, tiled=True)  92.5 us
    all_gather x1, waiting for transfers between devices, fetch_mlp(): lax.all_gather(down_weight, 'shard', axis=0, tiled=True)  76.7 us
  transfers between devices with their start and end apart: 19, of which 15 were waited for; matrix products, arithmetic and copies ran while one was open for 21% of the time, Pallas kernels for 0%

commit v1 on v0

--- a/solution.py
+++ b/solution.py
@@ -7,6 +7,18 @@
 QBLOCK = 512
 EPSILON = 1e-05
 MASKED_SCORE = -1e30
+
+
+def cut_along(value, dim, size):
+    dims = value.shape
+    blocks = value.reshape(*dims[:dim], size, dims[dim] // size, *dims[dim + 1 :])
+    return jnp.moveaxis(blocks, dim, 0)
+
+
+def laid_out(pieces, dim):
+    pieces = jnp.moveaxis(pieces, 0, dim)
+    shape = pieces.shape
+    return pieces.reshape(*shape[:dim], shape[dim] * shape[dim + 1], *shape[dim + 2 :])
 
 
 def layer_norm(hidden, gain, shift):
@@ -142,7 +154,14 @@
     normed_one, norm_pull_one = jax.vjp(layer_norm, hidden, gains[0], biases[0])
     inputs_one = normed_one.astype(jnp.bfloat16)
     projected = contract("cfd,jde->jcfe", inputs_one, project_all).astype(jnp.bfloat16)
-    by_heads = lax.all_to_all(projected, "seq", split_axis=3, concat_axis=2, tiled=True)
+    size, index = (lax.axis_size("seq"), lax.axis_index("seq"))
+    blocks = cut_along(projected, 3, size)
+    outs = [blocks[index]]
+    for step in range(1, size):
+        sent = blocks[(index + step) % size]
+        outs.append(lax.ppermute(sent, "seq", [(i, (i + step) % size) for i in range(size)]))
+    blocks = jnp.stack(outs)[(index - jnp.arange(size)) % size]
+    by_heads = laid_out(blocks, 2)
     queries = split_heads(by_heads[0])
     key_rows = split_heads(by_heads[1])
     value_rows = split_heads(by_heads[2])

time: 1750 us -> 1750 us (level)
    all_to_all x1 -> x0, waiting for transfers between devices: 69.5 us -> none  [body(): lax.all_to_all(projected, 'seq', split_axis=3, concat_axis=2, tiled=True)]
    ppermute x0 -> x3, waiting for transfers between devices: none -> 47.8 us  [body(): lax.ppermute(sent, 'seq', [(i, (i + step) % size) for i in range(size)])]
    unnamed x214 -> x218, local copies, waits for them, and re-layouts: 146 us -> 147 us
  transfers between devices with their start and end apart: 19 -> 21, of which waited for: 15 -> 18; matrix products, arithmetic and copies ran while one was open for 21% -> 21% of each run, Pallas kernels for 0% -> 0%
where the time goes in v1:
time: 1750 us; the launch traced here: 1740 us
  waiting for transfers between devices  1100 us (63%)
  matrix products  221 us (13%)
  local copies, waits for them, and re-layouts  217 us (12%)
  blocking collectives  104 us (6%)
  other arithmetic  69.8 us (4%)
    psum x1, waiting for transfers between devices, body(): lax.psum(project_share.astype(jnp.bfloat16), 'seq').astype(jnp.float32)  297 us
    dot_general x38, matrix products, contract(): return jnp.einsum(form, left, right, preferred_element_type=jnp.float32)  219 us
    unnamed x218, local copies, waits for them, and re-layouts  147 us
    reduce_scatter x1, waiting for transfers between devices, body(): lax.psum_scatter(grad_down.astype(jnp.bfloat16), 'shard', scatter_dimensi...  130 us
    reduce_scatter x1, waiting for transfers between devices, body(): lax.psum_scatter(grad_up.astype(jnp.bfloat16), 'shard', scatter_dimension...  130 us
    all_gather x1, waiting for transfers between devices, fetch_mlp(): lax.all_gather(up_weight, 'shard', axis=0, tiled=True)  96 us
    unnamed x20, waiting for transfers between devices  95.6 us
    all_gather x1, waiting for transfers between devices, fetch_mlp(): lax.all_gather(down_weight, 'shard', axis=0, tiled=True)  76.7 us
  transfers between devices with their start and end apart: 21, of which 18 were waited for; matrix products, arithmetic and copies ran while one was open for 21% of the time, Pallas kernels for 0%

profile of v1, /device:TPU:0, one launch (start us, length us, event | category | flops | bytes accessed | tf_op | source)
XLA Modules:
  0.0 1739.8 jit_solution(7159831616085723785)
XLA Ops:
  11.2 10.4 all-gather
  21.7 9.2 all-gather.1
  31.8 59.6 %all-gather.9.cloned.1.call-done = bf16[3,1536,1536]{2,1,0:T(8,128)(2,1)} async-done(((bf16[3,192,1536]{2,1,0:T(8,128)(2,1)}), bf16[3,1536,1536]{2,1,0:T(8,128)(2,1)}) %all-gather.9.cloned.1.call-update) | async-done | bytes 14155792 | tf_op jit(solution)/shard_map/all_gather | solution.py:113
  91.4 10.3 fusion.27
  118.2 10.6 collective-permute-done.2
  128.8 13.7 collective-permute-done
  142.5 23.5 %collective-permute-done.1 = bf16[3,1,256,384]{3,2,0,1:T(8,128)(2,1)S(1)} collective-permute-done((bf16[3,1,256,384]{3,2,0,1:T(8,128)(2,1)S(1)}, bf16[3,1,256,384]{3,2,0,1:T(8,128)(2,1)S(1)}, u32[]{:S(2)}, u32[]{:S(2)}) %collective-permute-start.1) | collective-permute-done | bytes 589856 | tf_op jit(solution)/shard_map/ppermute | solution.py:162
  216.9 12.0 all-to-all-done
  257.6 96.0 %all-gather.17.cloned.1.call-done = bf16[1536,6144]{1,0:T(8,128)(2,1)} async-done(((bf16[192,6144]{1,0:T(8,128)(2,1)}), bf16[1536,6144]{1,0:T(8,128)(2,1)}) %all-gather.17.cloned.1.call-update) | async-done | bytes 18874384 | tf_op jit(solution)/shard_map/all_gather | solution.py:129
  353.6 23.7 %multiply_convert_fusion.2 = (bf16[256,6144]{1,0:T(8,128)(2,1)}, f32[256,6144]{1,0:T(8,128)}, f32[256,6144]{1,0:T(8,128)}) fusion(bf16[1536,6144]{1,0:T(8,128)(2,1)} %all-gather.17.cloned.1.call-done, f32[1,256,1536]{2,1,0:T(8,128)S(1)} %get-tuple-element.196, f32[1536]{0:T(1024)S(1)} %get-tuple-element.161, f32[1536]{0:T(1024)S(1)} %get-tuple-element.210, ...), kind=kOutput, calls=%fused_computation.32 | convolution fusion | flops 4936040448 | bytes 36190208 | tf_op jit(solution)/shard_map/cfd,dk->cfk/dot_general | solution.py:35
  377.3 76.7 %all-gather.19.cloned.1.call-done = bf16[6144,1536]{1,0:T(8,128)(2,1)} async-done(((bf16[768,1536]{1,0:T(8,128)(2,1)}), bf16[6144,1536]{1,0:T(8,128)(2,1)}) %all-gather.19.cloned.1.call-update) | async-done | bytes 18874384 | tf_op jit(solution)/shard_map/all_gather | solution.py:130
  453.9 15.0 add_convert_fusion
  468.9 10.7 fusion.57
  513.5 24.3 %all-reduce.7.cloned.1.call-done = bf16[2,64,1536]{2,1,0:T(8,128)(2,1)} async-done(((bf16[2,64,1536]{2,1,0:T(8,128)(2,1)}), bf16[2,64,1536]{2,1,0:T(8,128)(2,1)}) %all-reduce.7.cloned.1.call-update) | async-done | bytes 393232 | tf_op jit(solution)/shard_map/psum | solution.py:231
  547.9 31.0 %copy.262 = bf16[3,1536,1536]{2,0,1:T(4,128)(2,1)} copy(bf16[3,1536,1536]{1,2,0:T(8,128)(2,1)} %pad_maximum_fusion) | data formatting | bytes 28311552
  578.8 17.0 copy.274
  620.8 18.2 %all-to-all-done.1 = bf16[4,2,49152]{2,1,0:T(2,128)(2,1)S(1)} async-done(((bf16[4,2,49152]{2,1,0:T(2,128)(2,1)}), bf16[4,2,49152]{2,1,0:T(2,128)(2,1)S(1)}, u32[]{:S(2)}, u32[]{:S(2)}) %all-to-all-start.1) | async-done | bytes 786464 | tf_op jit(solution)/shard_map/all_to_all | solution.py:253
  710.2 72.8 %all_to_all.45 = bf16[3,1,1024,384]{3,0,1,2:T(4,128)(2,1)S(1)} all-to-all(bf16[3,1,1024,384]{3,0,1,2:T(4,128)(2,1)S(1)} %pad_maximum_fusion.1), channel_id=1, replica_groups=mesh['seq'=4,'shard'=8] {'seq'}, dimensions={2} | all-to-all | bytes 4718592 | tf_op jit(solution)/shard_map/all_to_all | solution.py:260
  798.0 31.0 %copy.260 = bf16[3,1536,1536]{2,0,1:T(4,128)(2,1)} copy(bf16[3,1536,1536]{1,2,0:T(8,128)(2,1)} %convert_bitcast_fusion) | data formatting | bytes 28311552
  828.9 17.0 copy.273
  858.4 12.8 convolution_convert_fusion.1
  871.3 11.4 convolution_convert_fusion
  906.9 40.3 %reduce-scatter.29.cloned.1.call-done = bf16[192,4608]{1,0:T(8,128)(2,1)} async-done(((bf16[1536,4608]{1,0:T(8,128)(2,1)}), bf16[192,4608]{1,0:T(8,128)(2,1)}) %reduce-scatter.29.cloned.1.call-update) | async-done | bytes 1769488
  958.0 46.9 %reduce-scatter.19.cloned.1.call-done = bf16[192,1536]{1,0:T(8,128)(2,1)} async-done(((bf16[1536,1536]{1,0:T(8,128)(2,1)}), bf16[192,1536]{1,0:T(8,128)(2,1)}) %reduce-scatter.19.cloned.1.call-update) | async-done | bytes 589840 | tf_op jit(solution)/shard_map/reduce_scatter | solution.py:243
  1004.9 57.8 %reduce-scatter.17.cloned.1.call-done = bf16[192,1536]{1,0:T(8,128)(2,1)} async-done(((bf16[1536,1536]{1,0:T(8,128)(2,1)}), bf16[192,1536]{1,0:T(8,128)(2,1)}) %reduce-scatter.17.cloned.1.call-update) | async-done | bytes 589840 | tf_op jit(solution)/shard_map/reduce_scatter | solution.py:271
  1062.7 129.9 %reduce-scatter.21.cloned.1.call-done = bf16[192,6144]{1,0:T(8,128)(2,1)} async-done(((bf16[1536,6144]{1,0:T(8,128)(2,1)}), bf16[192,6144]{1,0:T(8,128)(2,1)}) %reduce-scatter.21.cloned.1.call-update) | async-done | bytes 2359312 | tf_op jit(solution)/shard_map/reduce_scatter | solution.py:208
  1192.7 130.1 %reduce-scatter.23.cloned.1.call-done = bf16[768,1536]{1,0:T(8,128)(2,1)} async-done(((bf16[6144,1536]{1,0:T(8,128)(2,1)}), bf16[768,1536]{1,0:T(8,128)(2,1)}) %reduce-scatter.23.cloned.1.call-update) | async-done | bytes 2359312 | tf_op jit(solution)/shard_map/reduce_scatter | solution.py:211
  1324.2 10.7 fusion.31
  1344.2 15.4 reduce-scatter.25.cloned.1.call-done
  1360.5 36.0 %reduce-scatter.27.cloned.1.call-done = bf16[192,3]{1,0:T(8,128)(2,1)} async-done(((bf16[1536,3]{1,0:T(8,128)(2,1)}), bf16[192,3]{1,0:T(8,128)(2,1)}) %reduce-scatter.27.cloned.1.call-update) | async-done | bytes 1168
  1397.3 11.9 all-reduce.2
  1415.2 297.1 %all-reduce.9.cloned.1.call-done = (bf16[3,192,1536]{1,2,0:T(8,128)(2,1)}, bf16[192,1536]{1,0:T(8,128)(2,1)}, bf16[1,192,1536]{1,2,0:T(8,128)(2,1)}, bf16[192,15...) async-done(((bf16[3,192,1536]{1,2,0:T(8,128)(2,1)}, bf16[192,1536]{1,0:T(8,128)(2,1)}, bf16[1,192,1536]{1,2,0:T(8,128)(2,1)}, ...) | async-done | bytes 8257552 | tf_op jit(solution)/shard_map/psum | solution.py:282
  (387 shorter events, 341.2 us)
Async XLA Ops:
  7.2 202.2 %copy-start = (bf16[1,64,1536]{2,1,0:T(8,128)(2,1)S(1)}, bf16[1,64,1536]{2,1,0:T(8,128)(2,1)}, u32[]{:S(2)}) copy-start(bf16[1,64,1536]{2,1,0:T(8,128)(2,1)} %param.24) | copy-start | bytes 589828
  7.2 84.2 %all-gather.9.cloned.1.call-start = ((), (), s32[]{:S(2)}) async-start(), calls=%async_computation.11 | async-start | bytes 15925248 | tf_op jit(solution)/shard_map/all_gather | solution.py:113
  7.9 201.5 %all-gather.13.cloned.1.call-start = ((), (), s32[]{:S(2)}) async-start(), calls=%async_computation.13 | async-start | bytes 15925248 | tf_op jit(solution)/shard_map/all_gather | solution.py:122
  8.7 221.6 %all-gather.11.cloned.1.call-start = ((), (), s32[]{:S(2)}) async-start(), calls=%async_computation.12 | async-start | bytes 5308416 | tf_op jit(solution)/shard_map/all_gather | solution.py:114
  9.4 243.8 %all-gather.15.cloned.1.call-start = ((), (), s32[]{:S(2)}) async-start(), calls=%async_computation.14 | async-start | bytes 5308416 | tf_op jit(solution)/shard_map/all_gather | solution.py:123
  10.0 343.6 %all-gather.17.cloned.1.call-start = ((), (), s32[]{:S(2)}) async-start(), calls=%async_computation.15 | async-start | bytes 21233664 | tf_op jit(solution)/shard_map/all_gather | solution.py:129
  10.6 443.3 %all-gather.19.cloned.1.call-start = ((), (), s32[]{:S(2)}) async-start(), calls=%async_computation.16 | async-start | bytes 21233664 | tf_op jit(solution)/shard_map/all_gather | solution.py:130
  31.2 70.5 %copy-start.65 = (f32[1536]{0:T(1024)}, f32[1536]{0:T(1024)S(1)}, u32[]{:S(2)}) copy-start(f32[1536]{0:T(1024)S(1)} %get-tuple-element.163) | copy-start | bytes 18436
  31.2 203.6 %copy-start.67 = (f32[1536]{0:T(1024)}, f32[1536]{0:T(1024)S(1)}, u32[]{:S(2)}) copy-start(f32[1536]{0:T(1024)S(1)} %get-tuple-element.209) | copy-start | bytes 18436
  31.2 203.6 %copy-start.83 = (f32[1536]{0:T(1024)}, f32[1536]{0:T(1024)S(1)}, u32[]{:S(2)}) copy-start(f32[1536]{0:T(1024)S(1)} %get-tuple-element.162) | copy-start | bytes 18436
  31.2 322.4 %copy-start.56 = (f32[1536]{0:T(1024)}, f32[1536]{0:T(1024)S(1)}, u32[]{:S(2)}) copy-start(f32[1536]{0:T(1024)S(1)} %get-tuple-element.161) | copy-start | bytes 18436
  31.4 70.3 %copy-start.70 = (f32[256]{0:T(256)}, f32[256]{0:T(256)S(1)}, u32[]{:S(2)}) copy-start(f32[256]{0:T(256)S(1)} %broadcast_multiply_fusion.2) | copy-start | bytes 3076
  31.8 70.0 %copy-start.76 = (f32[256]{0:T(256)}, f32[256]{0:T(256)S(1)}, u32[]{:S(2)}) copy-start(f32[256]{0:T(256)S(1)} %fusion.53) | copy-start | bytes 3076
  31.8 69.9 %copy-start.72 = (f32[256]{0:T(256)}, f32[256]{0:T(256)S(1)}, u32[]{:S(2)}) copy-start(f32[256]{0:T(256)S(1)} %fusion.100) | copy-start | bytes 3076
  111.7 17.1 collective-permute-start.2
  115.1 27.5 %collective-permute-start = (bf16[3,1,256,384]{3,2,0,1:T(8,128)(2,1)S(1)}, bf16[3,1,256,384]{3,2,0,1:T(8,128)(2,1)S(1)}, u32[]{:S(2)}, u32[]{:S(2)}) collective-permute-start(bf16[3,1,256,384]{3,2,0,1:T(8,128)(2,1)S(1)} %bitcast.393), channel_id=1, source_target_pairs={{0,8},{8,16},{16,24},{24,0},{1,9},{9,17},{17,25},{25,1},{2,10},{10... | collective-permute-start | bytes 1769480 | tf_op jit(solution)/shard_map/ppermute | solution.py:162
  115.1 51.0 %collective-permute-start.1 = (bf16[3,1,256,384]{3,2,0,1:T(8,128)(2,1)S(1)}, bf16[3,1,256,384]{3,2,0,1:T(8,128)(2,1)S(1)}, u32[]{:S(2)}, u32[]{:S(2)}) collective-permute-start(bf16[3,1,256,384]{3,2,0,1:T(8,128)(2,1)S(1)} %bitcast.392), channel_id=1, source_target_pairs={{0,16},{8,24},{16,0},{24,8},{1,17},{9,25},{17,1},{25,9},{2,18},{10... | collective-permute-start | bytes 1769480 | tf_op jit(solution)/shard_map/ppermute | solution.py:162
  205.5 23.3 %all-to-all-start = ((bf16[4,2,49152]{2,1,0:T(2,128)(2,1)}), bf16[4,2,49152]{2,1,0:T(2,128)(2,1)S(1)}, u32[]{:S(2)}, u32[]{:S(2)}) async-start(bf16[4,2,49152]{2,1,0:T(2,128)(2,1)} %reshape.1025), calls=%async_computation | async-start | bytes 1572864 | tf_op jit(solution)/shard_map/all_to_all | solution.py:169
  209.4 328.4 %all-reduce.7.cloned.1.call-start = ((), (), s32[]{:S(2)}) async-start(), calls=%async_computation.17 | async-start | bytes 786432 | tf_op jit(solution)/shard_map/psum | solution.py:231
  243.0 249.0 %copy-start.58 = (f32[24,256]{1,0:T(8,128)}, f32[24,256]{1,0:T(8,128)S(1)}, u32[]{:S(2)}) copy-start(f32[24,256]{1,0:T(8,128)S(1)} %get-tuple-element.193) | copy-start | bytes 73732
  257.3 222.4 %copy-start.9 = (f32[1,256,1536]{2,1,0:T(8,128)}, f32[1,256,1536]{2,1,0:T(8,128)S(1)}, u32[]{:S(2)}) copy-start(f32[1,256,1536]{2,1,0:T(8,128)S(1)} %get-tuple-element.196) | copy-start | bytes 4718596
  500.7 397.0 %reduce-scatter.31.cloned.1.call-start = ((), (), s32[]{:S(2)}) async-start(), calls=%async_computation.25 | async-start | bytes 15925248
  617.0 22.0 %all-to-all-start.1 = ((bf16[4,2,49152]{2,1,0:T(2,128)(2,1)}), bf16[4,2,49152]{2,1,0:T(2,128)(2,1)S(1)}, u32[]{:S(2)}, u32[]{:S(2)}) async-start(bf16[4,2,49152]{2,1,0:T(2,128)(2,1)} %reshape.1027), calls=%async_computation.1 | async-start | bytes 1572864 | tf_op jit(solution)/shard_map/all_to_all | solution.py:253
  620.7 326.5 %reduce-scatter.29.cloned.1.call-start = ((), (), s32[]{:S(2)}) async-start(), calls=%async_computation.24 | async-start | bytes 15925248
  846.0 158.9 %reduce-scatter.19.cloned.1.call-start = ((), (), s32[]{:S(2)}) async-start(), calls=%async_computation.19 | async-start | bytes 5308416 | tf_op jit(solution)/shard_map/reduce_scatter | solution.py:243
  851.3 211.4 %reduce-scatter.17.cloned.1.call-start = ((), (), s32[]{:S(2)}) async-start(), calls=%async_computation.18 | async-start | bytes 5308416 | tf_op jit(solution)/shard_map/reduce_scatter | solution.py:271
  857.7 335.0 %reduce-scatter.21.cloned.1.call-start = ((), (), s32[]{:S(2)}) async-start(), calls=%async_computation.20 | async-start | bytes 21233664 | tf_op jit(solution)/shard_map/reduce_scatter | solution.py:208
  871.2 451.5 %reduce-scatter.23.cloned.1.call-start = ((), (), s32[]{:S(2)}) async-start(), calls=%async_computation.21 | async-start | bytes 21233664 | tf_op jit(solution)/shard_map/reduce_scatter | solution.py:211
  882.7 476.9 %reduce-scatter.25.cloned.1.call-start = ((), (), s32[]{:S(2)}) async-start(), calls=%async_computation.22 | async-start | bytes 442368
  896.3 500.2 %reduce-scatter.27.cloned.1.call-start = ((), (), s32[]{:S(2)}) async-start(), calls=%async_computation.23 | async-start | bytes 442368
  897.4 814.9 %all-reduce.9.cloned.1.call-start = ((), (), s32[]{:S(2)}) async-start(), calls=%async_computation.26 | async-start | bytes 18087936 | tf_op jit(solution)/shard_map/psum | solution.py:282
  1342.5 67.9 %copy-start.18 = (bf16[192,3,1536]{2,1,0:T(4,128)(2,1)S(1)}, bf16[192,3,1536]{2,1,0:T(4,128)(2,1)}, u32[]{:S(2)}) copy-start(bf16[192,3,1536]{2,1,0:T(4,128)(2,1)} %copy-done.17) | copy-start | bytes 5308420
  (85 other events, 555.6 us)
Sparse Core Ops, SparseCore 0:
  9.9 81.4 all-gather.8
  93.3 78.6 all-gather.12
  173.8 38.7 all-gather.10
  214.4 38.7 all-gather.14
  254.9 98.5 all-gather.16
  355.3 98.5 all-gather.18
  500.8 36.9 all-reduce.6
  596.0 101.5 reduce-scatter.30
  846.1 101.0 reduce-scatter.28
  951.1 53.7 reduce-scatter.18
  1008.9 53.7 reduce-scatter.16
  1066.2 126.4 reduce-scatter.20
  1196.3 126.4 reduce-scatter.22
  1325.7 33.8 reduce-scatter.24
  1362.5 33.8 reduce-scatter.26
  1400.1 312.1 all-reduce.8
